TPU v7x, 32 devices: a whole 2x2x4 slice. The times are simulated.
32 devices in a mesh: sec: 2 (over core), var: 4 (over z), trait: 4 (over y, x).
Axes of the slice: x: 2, y: 2, z: 4, core: 2. Of those that a mesh axis runs over, the one named last changes fastest.
Arguments:
- z_typed: bfloat16 [32768, 512], P(('sec', 'var'), 'trait'), may hold values from -6 to 6
- band_inverse: bfloat16 [256, 128, 384], P(('sec', 'var')), may hold values from -0.3125 to 0.3125
- ld_untyped: bfloat16 [512, 128, 512], P(('sec', 'var')), may hold values from -0.375 to 0.375
- trait_mix: bfloat16 [512, 512], replicated, may hold values from -0.25 to 0.25
- win_start: int32 [512], P(('sec', 'var')), may hold values from 0 to 255, as said below
- win_count: int32 [512], P(('sec', 'var')), may hold values from 1 to 4, as said below
Outputs:
- imputed_mixed: bfloat16 [65536, 512], P(('sec', 'var'), 'trait')
Inputs may be any that keep to these rules, and one draw needn't show every extreme that they name: Windows follow chromosome order: within the 64 untyped blocks of one index g of sec+var, win_start never falls, and every window lies in typed blocks g * 32 - 32 to (g + 1) * 32 + 31; the first window of each index starts at its lower end (or at 0) and the last one ends at its upper end (or at the chromosome's end). win_start + win_count never exceeds 256.
All inputs are finite; a program needn't handle non-finite values.
Results may differ from a plain program's by a relative error of at most 0.0057.
Values may be sent and summed in bfloat16 or wider, within the bound.
A program may use at most 64 MiB of HBM per device.

v0:
```python
import jax
import jax.numpy as jnp
from jax import lax
from jax.sharding import PartitionSpec as P

BLK = 128
WIN = 4


def padded_2(cells, sides, width):
    for axis, dim in sides:
        count = lax.axis_size(axis)
        ends = count - 1
        head = lax.slice_in_dim(cells, 0, width, axis=dim)
        tail = lax.slice_in_dim(cells, cells.shape[dim] - width, cells.shape[dim], axis=dim)
        cells = jnp.concatenate(
            [
                lax.ppermute(tail, axis, [(i, (i + 1) % count) for i in range(ends)]),
                cells,
                lax.ppermute(head, axis, [((i + 1) % count, i) for i in range(ends)]),
            ],
            axis=dim,
        )
    return cells


def on_device(z_typed, band_inverse, ld_untyped, trait_mix, win_start, win_count):
    trait_cols = z_typed.shape[1]
    typed_blocks = z_typed.shape[0] // BLK
    padded = padded_2(z_typed, ((("sec", "var"), 0),), BLK)
    stacked = jnp.concatenate(
        [
            padded[k * BLK : (k + typed_blocks) * BLK].reshape(typed_blocks, BLK, trait_cols)
            for k in range(3)
        ],
        axis=1,
    )
    whitened = jnp.einsum(
        "bij,bjc->bic", band_inverse, stacked, preferred_element_type=jnp.float32
    ).astype(jnp.bfloat16)
    whitened_rows = whitened.reshape(typed_blocks * BLK, trait_cols)
    column_start = lax.axis_index("trait") * trait_cols
    mix_cols = lax.dynamic_slice_in_dim(trait_mix, column_start, trait_cols, 1)
    mixed_sums = jnp.dot(
        lax.all_gather(whitened_rows, "trait", axis=1, tiled=True),
        mix_cols,
        preferred_element_type=jnp.float32,
    )
    mixed = mixed_sums.astype(jnp.bfloat16).reshape(typed_blocks, BLK, trait_cols)
    window_steps = jnp.arange(WIN, dtype=jnp.int32)
    usable = window_steps[None, :] < win_count[:, None]
    untyped_blocks = win_start.shape[0]
    extended = padded_2(mixed, ((("sec", "var"), 0),), typed_blocks)
    local_first = win_start - lax.axis_index(("sec", "var")) * typed_blocks + typed_blocks
    wanted = jnp.clip(local_first[:, None] + window_steps[None, :], 0, 3 * typed_blocks - 1)
    picked = extended[wanted]
    chosen = jnp.where(usable[:, :, None, None], picked, jnp.zeros_like(picked))
    window_rows = chosen.reshape(untyped_blocks, WIN * BLK, trait_cols)
    imputed = jnp.einsum(
        "uij,ujc->uic", ld_untyped, window_rows, preferred_element_type=jnp.float32
    ).astype(jnp.bfloat16)
    return imputed.reshape(untyped_blocks * BLK, trait_cols)


def solution(mesh):
    in_specs = (
        P(("sec", "var"), "trait"),
        P(("sec", "var"), None, None),
        P(("sec", "var"), None, None),
        P(),
        P(("sec", "var")),
        P(("sec", "var")),
    )
    out_specs = P(("sec", "var"), "trait")
    return jax.shard_map(
        on_device, mesh=mesh, in_specs=in_specs, out_specs=out_specs, check_vma=False
    )
```

profile of v0, /device:TPU:1, one launch (start us, length us, event | category | flops | bytes accessed | tf_op | source)
XLA Modules:
  0.0 155.3 jit_solution(13202590645966387726)
XLA Ops:
  6.5 0.0 copy-start
  6.5 0.0 all-gather.2.cloned.1.call-start
  6.5 0.9 fusion.12
  7.5 4.1 %collective-permute-start = (bf16[128,128]{1,0:T(8,128)(2,1)S(1)}, bf16[128,128]{1,0:T(8,128)(2,1)S(1)}, u32[]{:S(2)}, u32[]{:S(2)}) collective-permute-start(bf16[128,128]{1,0:T(8,128)(2,1)S(1)} %get-tuple-element.7), channel_id=1, source_target_pairs={{0,4},{4,8},{8,12},{12,16},{16,20},{20,24},{24,28},{1,5},{5,9},{9,... | collective-permute-start | bytes 98312 | tf_op jit(solution)/shard_map/ppermute | solution.py:18
  11.6 4.5 %collective-permute-start.1 = (bf16[128,128]{1,0:T(8,128)(2,1)S(1)}, bf16[128,128]{1,0:T(8,128)(2,1)S(1)}, u32[]{:S(2)}, u32[]{:S(2)}) collective-permute-start(bf16[128,128]{1,0:T(8,128)(2,1)S(1)} %get-tuple-element.8), channel_id=1, source_target_pairs={{4,0},{8,4},{12,8},{16,12},{20,16},{24,20},{28,24},{5,1},{9,5},{13... | collective-permute-start | bytes 98312 | tf_op jit(solution)/shard_map/ppermute | solution.py:20
  16.1 0.0 collective-permute-done
  16.1 1.0 collective-permute-done.1
  17.1 1.7 %pad_maximum_fusion.2 = (bf16[4096,128]{1,0:T(8,128)(2,1)S(1)}, bf16[4096,128]{1,0:T(8,128)(2,1)S(1)}) fusion(bf16[4096,128]{1,0:T(8,128)(2,1)} %param.6, bf16[128,128]{1,0:T(8,128)(2,1)S(1)} %collective-permute-done, bf16[128,128]{1,0:T(8,128)(2,1)S(1)} %collective-permute-done.1), kind=kLoop, calls=%fused_computation.13 | loop fusion | flops 4194304 | bytes 3211264 | tf_op jit(solution)/shard_map/concatenate | solution.py:16
  18.8 0.0 copy-done
  18.8 3.2 %fusion.6 = bf16[32,128,128]{1,2,0:T(8,128)(2,1)} fusion(bf16[32,128,384]{2,1,0:T(8,128)(2,1)S(1)} %copy-done, bf16[32,128,128]{2,1,0:T(8,128)(2,1)S(1)} %bitcast.26, bf16[32,128,128]{2,1,0:T(8,128)(2,1)} %bitcast.24, bf16[32,128,128]{2,1,0:T(8,128)(2,1)S(1)} %bitcast.25), kind=kOutput, calls=%fused_computation.11 | convolution fusion | flops 412614656 | bytes 7340032 | tf_op jit(solution)/shard_map/bij,bjc->bic/dot_general | solution.py:38
  22.1 0.0 copy-start.1
  22.1 0.0 copy-start.2
  22.1 0.0 all-gather.2.cloned.1.call-update
  22.1 53.9 %all-gather.2.cloned.1.call-done = bf16[4096,512]{1,0:T(8,128)(2,1)} async-done(((bf16[4096,128]{1,0:T(8,128)(2,1)}), bf16[4096,512]{1,0:T(8,128)(2,1)}) %all-gather.2.cloned.1.call-update) | async-done | bytes 4194320 | tf_op jit(solution)/shard_map/all_gather | solution.py:45
  76.0 4.4 %convolution_convert_fusion = bf16[4096,128]{1,0:T(8,128)(2,1)} fusion(bf16[4096,512]{1,0:T(8,128)(2,1)} %all-gather.2.cloned.1.call-done, bf16[512,512]{1,0:T(8,128)(2,1)} %param.9, s32[]{:T(128)S(6)} %select_n.18), kind=kOutput, calls=%fused_computation.2 | convolution fusion | flops 537395200 | bytes 5373956 | tf_op jit(solution)/shard_map/dot_general | solution.py:44
  80.4 5.7 %collective-permute-start.3 = (bf16[32,128,128]{2,1,0:T(8,128)(2,1)}, bf16[32,128,128]{2,1,0:T(8,128)(2,1)}, u32[]{:S(2)}, u32[]{:S(2)}) collective-permute-start(bf16[32,128,128]{2,1,0:T(8,128)(2,1)} %bitcast.5), channel_id=1, source_target_pairs={{4,0},{8,4},{12,8},{16,12},{20,16},{24,20},{28,24},{5,1},{9,5},{13... | collective-permute-start | bytes 3145736 | tf_op jit(solution)/shard_map/ppermute | solution.py:20
  86.1 1.9 %collective-permute-start.2 = (bf16[32,128,128]{2,1,0:T(8,128)(2,1)}, bf16[32,128,128]{2,1,0:T(8,128)(2,1)}, u32[]{:S(2)}, u32[]{:S(2)}) collective-permute-start(bf16[32,128,128]{2,1,0:T(8,128)(2,1)} %bitcast.5), channel_id=1, source_target_pairs={{0,4},{4,8},{8,12},{12,16},{16,20},{20,24},{24,28},{1,5},{5,9},{9,... | collective-permute-start | bytes 3145736 | tf_op jit(solution)/shard_map/ppermute | solution.py:18
  88.0 0.0 copy-done.1
  88.1 0.1 iota_compare_fusion
  88.1 0.1 broadcast_in_dim.21
  88.3 0.0 copy-done.2
  88.3 0.1 compare_select_fusion
  88.4 0.1 reshape.93
  88.5 19.8 %collective-permute-done.3 = bf16[32,128,128]{2,1,0:T(8,128)(2,1)} collective-permute-done((bf16[32,128,128]{2,1,0:T(8,128)(2,1)}, bf16[32,128,128]{2,1,0:T(8,128)(2,1)}, u32[]{:S(2)}, u32[]{:S(2)}) %collective-permute-start.3) | collective-permute-done | bytes 1048608 | tf_op jit(solution)/shard_map/ppermute | solution.py:20
  108.3 12.4 %collective-permute-done.2 = bf16[32,128,128]{2,1,0:T(8,128)(2,1)} collective-permute-done((bf16[32,128,128]{2,1,0:T(8,128)(2,1)}, bf16[32,128,128]{2,1,0:T(8,128)(2,1)}, u32[]{:S(2)}, u32[]{:S(2)}) %collective-permute-start.2) | collective-permute-done | bytes 1048608 | tf_op jit(solution)/shard_map/ppermute | solution.py:18
  120.7 3.3 %pad_maximum_fusion = bf16[96,128,128]{2,1,0:T(8,128)(2,1)} fusion(bf16[32,128,128]{2,1,0:T(8,128)(2,1)} %collective-permute-done.3, bf16[32,128,128]{2,1,0:T(8,128)(2,1)} %bitcast.5, bf16[32,128,128]{2,1,0:T(8,128)(2,1)} %collective-permute-done.2), kind=kLoop, calls=%fused_computation.9 | loop fusion | flops 3145728 | bytes 6291456 | tf_op jit(solution)/shard_map/concatenate | solution.py:16
  123.9 10.5 %gather_fusion = bf16[256,128,128]{2,1,0:T(8,128)(2,1)} fusion(bf16[96,128,128]{2,1,0:T(8,128)(2,1)} %pad_maximum_fusion, s32[1024]{0:T(1024)S(1)} %pad_clamp_fusion), kind=kCustom, calls=%fused_computation | custom fusion | bytes 16778240 | tf_op jit(solution)/shard_map/gather | solution.py:56
  134.4 7.0 %bitcast_select_fusion = bf16[64,512,128]{2,1,0:T(8,128)(2,1)S(1)} fusion(pred[64,512]{1,0:T(8,128)(4,1)S(1)} %bitcast.28, bf16[64,512,128]{2,1,0:T(8,128)(2,1)} %bitcast.23), kind=kLoop, calls=%fused_computation.1 | loop fusion | flops 4194304 | bytes 16809984 | tf_op jit(solution)/shard_map/jit(_where)/select_n | solution.py:57
  141.5 7.0 %convolution_convert_fusion.1 = bf16[64,128,128]{1,2,0:T(8,128)(2,1)} fusion(bf16[64,128,512]{2,1,0:T(8,128)(2,1)} %param.8, bf16[64,512,128]{2,1,0:T(8,128)(2,1)S(1)} %bitcast_select_fusion), kind=kOutput, calls=%fused_computation.10 | convolution fusion | flops 1074790400 | bytes 18874368 | tf_op jit(solution)/shard_map/uij,ujc->uic/dot_general | solution.py:59
  (3 shorter events, 0.0 us)
Async XLA Ops:
  6.5 12.3 %copy-start = (bf16[32,128,384]{2,1,0:T(8,128)(2,1)S(1)}, bf16[32,128,384]{2,1,0:T(8,128)(2,1)}, u32[]{:S(2)}) copy-start(bf16[32,128,384]{2,1,0:T(8,128)(2,1)} %param.7) | copy-start | bytes 9437188
  6.5 69.5 %all-gather.2.cloned.1.call-start = ((), (), s32[]{:S(2)}) async-start(), calls=%async_computation | async-start | bytes 5242880 | tf_op jit(solution)/shard_map/all_gather | solution.py:45
  7.5 8.7 %collective-permute-start = (bf16[128,128]{1,0:T(8,128)(2,1)S(1)}, bf16[128,128]{1,0:T(8,128)(2,1)S(1)}, u32[]{:S(2)}, u32[]{:S(2)}) collective-permute-start(bf16[128,128]{1,0:T(8,128)(2,1)S(1)} %get-tuple-element.7), channel_id=1, source_target_pairs={{0,4},{4,8},{8,12},{12,16},{16,20},{20,24},{24,28},{1,5},{5,9},{9,... | collective-permute-start | bytes 98312 | tf_op jit(solution)/shard_map/ppermute | solution.py:18
  11.6 5.5 %collective-permute-start.1 = (bf16[128,128]{1,0:T(8,128)(2,1)S(1)}, bf16[128,128]{1,0:T(8,128)(2,1)S(1)}, u32[]{:S(2)}, u32[]{:S(2)}) collective-permute-start(bf16[128,128]{1,0:T(8,128)(2,1)S(1)} %get-tuple-element.8), channel_id=1, source_target_pairs={{4,0},{8,4},{12,8},{16,12},{20,16},{24,20},{28,24},{5,1},{9,5},{13... | collective-permute-start | bytes 98312 | tf_op jit(solution)/shard_map/ppermute | solution.py:20
  22.1 66.0 %copy-start.1 = (s32[64]{0:T(128)S(1)}, s32[64]{0:T(128)}, u32[]{:S(2)}) copy-start(s32[64]{0:T(128)} %param.11) | copy-start | bytes 772
  22.1 66.2 %copy-start.2 = (s32[64]{0:T(128)S(1)}, s32[64]{0:T(128)}, u32[]{:S(2)}) copy-start(s32[64]{0:T(128)} %param.10) | copy-start | bytes 772
  80.4 27.9 %collective-permute-start.3 = (bf16[32,128,128]{2,1,0:T(8,128)(2,1)}, bf16[32,128,128]{2,1,0:T(8,128)(2,1)}, u32[]{:S(2)}, u32[]{:S(2)}) collective-permute-start(bf16[32,128,128]{2,1,0:T(8,128)(2,1)} %bitcast.5), channel_id=1, source_target_pairs={{4,0},{8,4},{12,8},{16,12},{20,16},{24,20},{28,24},{5,1},{9,5},{13... | collective-permute-start | bytes 3145736 | tf_op jit(solution)/shard_map/ppermute | solution.py:20
  86.1 34.6 %collective-permute-start.2 = (bf16[32,128,128]{2,1,0:T(8,128)(2,1)}, bf16[32,128,128]{2,1,0:T(8,128)(2,1)}, u32[]{:S(2)}, u32[]{:S(2)}) collective-permute-start(bf16[32,128,128]{2,1,0:T(8,128)(2,1)} %bitcast.5), channel_id=1, source_target_pairs={{0,4},{4,8},{8,12},{12,16},{16,20},{20,24},{24,28},{1,5},{5,9},{9,... | collective-permute-start | bytes 3145736 | tf_op jit(solution)/shard_map/ppermute | solution.py:18
Sparse Core Ops, SparseCore 0:
  22.2 53.7 all-gather.1
where the time goes:
time: 156 us; the launch traced here: 155 us
  waiting for transfers between devices  87.1 us (56%)
  starting transfers between devices  16.2 us (10%)
  matrix products  14.7 us (9%)
  between operations  13.5 us (9%)
  other arithmetic  12.1 us (8%)
  local copies, waits for them, and re-layouts  11.7 us (8%)
    all_gather x1, waiting for transfers between devices, on_device(): lax.all_gather(whitened_rows, 'trait', axis=1, tiled=True)  53.9 us
    ppermute x2, waiting for transfers between devices, padded_2(): lax.ppermute(head, axis, [((i + 1) % count, i) for i in range(ends)])  20.7 us
    ppermute x2, waiting for transfers between devices, padded_2(): lax.ppermute(tail, axis, [(i, (i + 1) % count) for i in range(ends)])  12.4 us
    gather x1, local copies, waits for them, and re-layouts, on_device(): picked = extended[wanted]  10.5 us
    ppermute x2, starting transfers between devices, padded_2(): lax.ppermute(head, axis, [((i + 1) % count, i) for i in range(ends)])  10.2 us
    dot_general x1, matrix products, on_device(): jnp.einsum('uij,ujc->uic', ld_untyped, window_rows, preferred_element_typ...  7.04 us
    select_n x1, other arithmetic, on_device(): chosen = jnp.where(usable[:, :, None, None], picked, jnp.zeros_like(picked))  7.01 us
    ppermute x2, starting transfers between devices, padded_2(): lax.ppermute(tail, axis, [(i, (i + 1) % count) for i in range(ends)])  6.06 us
  transfers between devices with their start and end apart: 5, of which 4 were waited for; matrix products, arithmetic and copies ran while one was open for 0% of the time, Pallas kernels for 0%

commit v1 on v0

v1 whole, which is shorter than its diff:
```python
import functools

import jax
import jax.numpy as jnp
from jax import lax
from jax.experimental import pallas as pl
from jax.experimental.pallas import tpu as pltpu
from jax.sharding import PartitionSpec as P

BLK = 128
WIN = 4
CHUNK_BLOCKS = 4
AHEAD = 2
UNTYPED_TILE = 8
MESH = pl.DeviceIdType.MESH


def mixed_kernel(
    chunks, blocks, groups, var_size,
    z_ref, band_ref, mix_ref, ext_ref,
    zb, bandv, w, mv, mx,
    z_sem, band_sem, mix_sem, own_sem, edge_send, edge_recv, xy_send, xy_recv, halo_send, halo_recv,
):
    t = lax.axis_index("trait")
    g = lax.axis_index("sec") * var_size + lax.axis_index("var")
    x_peer = t + 1 - 2 * lax.rem(t, 2)
    y_peer = t + 2 - 4 * (t // 2)
    far_peer = x_peer + y_peer - t
    x_dev, y_dev = {"trait": x_peer}, {"trait": y_peer}
    right = {"sec": (g + 1) // var_size, "var": lax.rem(g + 1, var_size)}
    left_g = lax.rem(g + groups - 1, groups)
    left = {"sec": left_g // var_size, "var": lax.rem(left_g, var_size)}
    has_left, has_right = g > 0, g < groups - 1
    rows = blocks * BLK
    chunk = CHUNK_BLOCKS * BLK
    half = chunk // 2

    barrier = pltpu.get_barrier_semaphore()

    def greet(device):
        pl.semaphore_signal(barrier, inc=1, device_id=device, device_id_type=MESH)

    greet(x_dev)
    greet(y_dev)
    pl.when(has_left)(lambda: greet(left))
    pl.when(has_right)(lambda: greet(right))

    def remote(src, dst, send, recv, device):
        return pltpu.make_async_remote_copy(
            src_ref=src, dst_ref=dst, send_sem=send, recv_sem=recv,
            device_id=device, device_id_type=MESH,
        )

    load_z = pltpu.make_async_copy(z_ref, zb.at[pl.ds(BLK, rows)], z_sem)
    load_z.start()
    order = [(i + 1) % chunks for i in range(chunks)]

    def load_band(c):
        part = pl.ds(c * CHUNK_BLOCKS, CHUNK_BLOCKS)
        return pltpu.make_async_copy(band_ref.at[part], bandv.at[part], band_sem.at[c])

    for c in order:
        load_band(c).start()
    columns = pl.ds(pl.multiple_of(t * BLK, BLK), BLK)
    load_mix = [
        pltpu.make_async_copy(
            mix_ref.at[pl.ds(pl.multiple_of(peer * BLK, BLK), BLK), columns],
            mv.at[pl.ds(j * BLK, BLK)],
            mix_sem.at[j],
        )
        for j, peer in enumerate((t, x_peer, y_peer, far_peer))
    ]
    for copy in load_mix:
        copy.start()

    @pl.when(jnp.logical_not(has_left))
    def _():
        zb[pl.ds(0, BLK), :] = jnp.zeros((BLK, BLK), zb.dtype)

    @pl.when(jnp.logical_not(has_right))
    def _():
        zb[pl.ds(rows + BLK, BLK), :] = jnp.zeros((BLK, BLK), zb.dtype)

    edge_right = remote(
        z_ref.at[pl.ds(rows - BLK, BLK)], zb.at[pl.ds(0, BLK)], edge_send.at[0], edge_recv.at[0], right
    )
    edge_left = remote(
        z_ref.at[pl.ds(0, BLK)], zb.at[pl.ds(rows + BLK, BLK)], edge_send.at[1], edge_recv.at[1], left
    )

    def whiten(c):
        load_band(c).wait()
        if c == chunks - 1:
            pl.when(has_right)(edge_left.wait_recv)
        if c == 0:
            pl.when(has_left)(edge_right.wait_recv)

        def one(i, carry):
            b = c * CHUNK_BLOCKS + i
            first = pl.multiple_of(b * BLK, BLK)
            sums = jnp.dot(bandv[b], zb[pl.ds(first, 3 * BLK), :], preferred_element_type=jnp.float32)
            w[0, pl.ds(first, BLK), :] = sums.astype(w.dtype)
            return carry

        lax.fori_loop(0, CHUNK_BLOCKS, one, 0)

    def own_sends(c):
        part = pl.ds(c * chunk, chunk)
        return (
            remote(w.at[0, part], w.at[1, part], xy_send.at[0, c], xy_recv.at[0, c], x_dev),
            remote(w.at[0, part], w.at[2, part], xy_send.at[1, c], xy_recv.at[1, c], y_dev),
        )

    def relays(c):
        lower, upper = pl.ds(c * chunk, half), pl.ds(c * chunk + half, half)
        return (
            remote(w.at[1, lower], w.at[3, lower], xy_send.at[2, c], xy_recv.at[2, c], y_dev),
            remote(w.at[2, upper], w.at[3, upper], xy_send.at[3, c], xy_recv.at[3, c], x_dev),
        )

    def halos(c):
        part = pl.ds(c * chunk, chunk)
        return (
            remote(mx.at[part], ext_ref.at[part], halo_send.at[0, c], halo_recv.at[0, c], right),
            remote(
                mx.at[part], ext_ref.at[pl.ds(2 * rows + c * chunk, chunk)],
                halo_send.at[1, c], halo_recv.at[1, c], left,
            ),
        )

    def keep(c):
        return pltpu.make_async_copy(
            mx.at[pl.ds(c * chunk, chunk)], ext_ref.at[pl.ds(rows + c * chunk, chunk)], own_sem.at[c]
        )

    def mix(c):
        part = pl.ds(c * chunk, chunk)
        all_traits = jnp.concatenate([w[j, part, :] for j in range(4)], axis=1)
        sums = jnp.dot(all_traits, mv[...], preferred_element_type=jnp.float32)
        mx[part, :] = sums.astype(mx.dtype)

    load_z.wait()
    for c in order[: AHEAD + 1]:
        whiten(c)
    pl.semaphore_wait(barrier, 2 + has_left.astype(jnp.int32) + has_right.astype(jnp.int32))
    pl.when(has_right)(edge_right.start)
    pl.when(has_left)(edge_left.start)
    for c in order[:AHEAD]:
        for copy in own_sends(c):
            copy.start()
    for copy in load_mix:
        copy.wait()
    for i in range(chunks + 1):
        if i < chunks:
            for copy in own_sends(order[i]):
                copy.wait_recv()
            for copy in relays(order[i]):
                copy.start()
            if i + AHEAD < chunks:
                for copy in own_sends(order[i + AHEAD]):
                    copy.start()
        if i >= 1:
            c = order[i - 1]
            for copy in relays(c):
                copy.wait_recv()
            mix(c)
            to_right, to_left = halos(c)
            pl.when(has_right)(to_right.start)
            pl.when(has_left)(to_left.start)
            keep(c).start()
        if i + AHEAD + 1 < chunks:
            whiten(order[i + AHEAD + 1])
    for c in order:
        for copy in own_sends(c) + relays(c):
            copy.wait_send()
        keep(c).wait()
        to_right, to_left = halos(c)

        @pl.when(has_right)
        def _():
            to_right.wait_send()
            to_left.wait_recv()

        @pl.when(has_left)
        def _():
            to_left.wait_send()
            to_right.wait_recv()

    pl.when(has_right)(edge_right.wait_send)
    pl.when(has_left)(edge_left.wait_send)


def mixed_with_neighbours(z_typed, band_inverse, trait_mix, groups, var_size):
    rows = z_typed.shape[0]
    blocks = rows // BLK
    chunks = blocks // CHUNK_BLOCKS
    dma = pltpu.SemaphoreType.DMA
    kind = z_typed.dtype
    return pl.pallas_call(
        functools.partial(mixed_kernel, chunks, blocks, groups, var_size),
        out_shape=jax.ShapeDtypeStruct((3 * rows, BLK), kind),
        in_specs=[pl.BlockSpec(memory_space=pl.ANY)] * 3,
        out_specs=pl.BlockSpec(memory_space=pl.ANY),
        scratch_shapes=[
            pltpu.VMEM((rows + 2 * BLK, BLK), kind),
            pltpu.VMEM(band_inverse.shape, kind),
            pltpu.VMEM((4, rows, BLK), kind),
            pltpu.VMEM((4 * BLK, BLK), kind),
            pltpu.VMEM((rows, BLK), kind),
            dma, dma((chunks,)), dma((4,)), dma((chunks,)),
            dma((2,)), dma((2,)),
            dma((4, chunks)), dma((4, chunks)),
            dma((2, chunks)), dma((2, chunks)),
        ],
        compiler_params=pltpu.CompilerParams(
            collective_id=0, has_side_effects=True, vmem_limit_bytes=16 * 1024 * 1024
        ),
        name="mixed_kernel",
    )(z_typed, band_inverse, trait_mix)


def impute_kernel(blocks, var_size, start_ref, count_ref, ext_ref, ld_ref, out_ref):
    g = lax.axis_index("sec") * var_size + lax.axis_index("var")
    tile = ld_ref.shape[0]
    first = pl.program_id(0) * tile
    for i in range(tile):
        start = start_ref[first + i] - (g - 1) * blocks
        count = count_ref[first + i]
        parts = []
        for s in range(WIN):
            block = ext_ref[jnp.clip(start + s, 0, 3 * blocks - 1)]
            parts.append(jnp.where(s < count, block, jnp.zeros_like(block)))
        window = jnp.concatenate(parts, axis=0)
        sums = jnp.dot(ld_ref[i], window, preferred_element_type=jnp.float32)
        out_ref[i] = sums.astype(out_ref.dtype)


def impute(ext, ld_untyped, win_start, win_count, var_size):
    untyped = ld_untyped.shape[0]
    total = ext.shape[0] // BLK
    cols = ext.shape[1]
    return pl.pallas_call(
        functools.partial(impute_kernel, total // 3, var_size),
        grid_spec=pltpu.PrefetchScalarGridSpec(
            num_scalar_prefetch=2,
            grid=(untyped // UNTYPED_TILE,),
            in_specs=[
                pl.BlockSpec((total, BLK, cols), lambda i, *_: (0, 0, 0)),
                pl.BlockSpec((UNTYPED_TILE,) + ld_untyped.shape[1:], lambda i, *_: (i, 0, 0)),
            ],
            out_specs=pl.BlockSpec((UNTYPED_TILE, BLK, cols), lambda i, *_: (i, 0, 0)),
        ),
        out_shape=jax.ShapeDtypeStruct((untyped, BLK, cols), ext.dtype),
        compiler_params=pltpu.CompilerParams(vmem_limit_bytes=24 * 1024 * 1024),
        name="impute_kernel",
    )(win_start, win_count, ext.reshape(total, BLK, cols), ld_untyped)


def on_device(groups, var_size, z_typed, band_inverse, ld_untyped, trait_mix, win_start, win_count):
    ext = mixed_with_neighbours(z_typed, band_inverse, trait_mix, groups, var_size)
    imputed = impute(ext, ld_untyped, win_start, win_count, var_size)
    return imputed.reshape(ld_untyped.shape[0] * BLK, z_typed.shape[1])


def solution(mesh):
    var_size = mesh.shape["var"]
    groups = mesh.shape["sec"] * var_size
    in_specs = (
        P(("sec", "var"), "trait"),
        P(("sec", "var"), None, None),
        P(("sec", "var"), None, None),
        P(),
        P(("sec", "var")),
        P(("sec", "var")),
    )
    return jax.shard_map(
        functools.partial(on_device, groups, var_size),
        mesh=mesh, in_specs=in_specs, out_specs=P(("sec", "var"), "trait"), check_vma=False,
    )
```

time: 156 us -> 66.1 us (0.42)
  waiting for transfers between devices: 87.1 us -> 0 us
  Pallas kernels: 0 us -> 58.3 us
  starting transfers between devices: 16.2 us -> 0 us
  matrix products: 14.7 us -> 0 us
  between operations: 13.5 us -> 0.04 us
  other arithmetic: 12.1 us -> 0 us
  local copies, waits for them, and re-layouts: 11.7 us -> 7.54 us
    pallas_call x0 -> x2, Pallas kernels: none -> 58.3 us  [the longest x1 52.6 us: mixed_with_neighbours(): pl.pallas_call(functools.partial(mixed_kernel, chunks, blocks, groups, va...]
    all_gather x1 -> x0, waiting for transfers between devices: 53.9 us -> none  [on_device(): lax.all_gather(whitened_rows, 'trait', axis=1, tiled=True)]
    ppermute x4 -> x0, waiting for transfers between devices: 33.1 us -> none  [the longest x2 20.7 us: padded_2(): lax.ppermute(head, axis, [((i + 1) % count, i) for i in range(ends)])]
    ppermute x4 -> x0, starting transfers between devices: 16.2 us -> none  [the longest x2 10.2 us: padded_2(): lax.ppermute(head, axis, [((i + 1) % count, i) for i in range(ends)])]
    dot_general x3 -> x0, matrix products: 14.7 us -> none  [the longest x1 7.04 us: on_device(): jnp.einsum('uij,ujc->uic', ld_untyped, window_rows, preferred_element_typ...]
    gather x1 -> x0, local copies, waits for them, and re-layouts: 10.5 us -> none  [on_device(): picked = extended[wanted]]
    unnamed x7 -> x12, local copies, waits for them, and re-layouts: 0.03 us -> 7.54 us
    select_n x2 -> x0, other arithmetic: 7.09 us -> none  [the longest x1 7.01 us: on_device(): chosen = jnp.where(usable[:, :, None, None], picked, jnp.zeros_like(picked))]
  transfers between devices with their start and end apart: 5 -> 0, of which waited for: 4 -> 0; matrix products, arithmetic and copies ran while one was open for 0% -> 0% of each run, Pallas kernels for 0% -> 0%
where the time goes in v1:
time: 66.1 us; the launch traced here: 65.9 us
  Pallas kernels  58.3 us (88%)
  local copies, waits for them, and re-layouts  7.54 us (11%)
    pallas_call x1, Pallas kernels, mixed_with_neighbours(): pl.pallas_call(functools.partial(mixed_kernel, chunks, blocks, groups, va...  52.6 us
    unnamed x12, local copies, waits for them, and re-layouts  7.54 us
    pallas_call x1, Pallas kernels, impute(): pl.pallas_call(functools.partial(impute_kernel, total // 3, var_size), gr...  5.63 us

profile of v1, /device:TPU:1, one launch (start us, length us, event | category | flops | bytes accessed | tf_op | source)
XLA Modules:
  0.0 65.9 jit_solution(3863361372088094207)
XLA Ops:
  0.0 0.0 copy-start.1
  0.0 1.9 %copy-done.1 = bf16[32,128,384]{2,1,0:T(8,128)(2,1)S(1)} copy-done((bf16[32,128,384]{2,1,0:T(8,128)(2,1)S(1)}, bf16[32,128,384]{2,1,0:T(8,128)(2,1)}, u32[]{:S(2)}) %copy-start.1) | copy-done | bytes 3145752
  1.9 0.0 copy-start.2
  1.9 1.2 %copy-done.2 = bf16[4096,128]{1,0:T(8,128)(2,1)S(1)} copy-done((bf16[4096,128]{1,0:T(8,128)(2,1)S(1)}, bf16[4096,128]{1,0:T(8,128)(2,1)}, u32[]{:S(2)}) %copy-start.2) | copy-done | bytes 1048600
  3.1 0.0 copy-start.3
  3.1 1.0 %copy-done.3 = bf16[512,512]{1,0:T(8,128)(2,1)S(1)} copy-done((bf16[512,512]{1,0:T(8,128)(2,1)S(1)}, bf16[512,512]{1,0:T(8,128)(2,1)}, u32[]{:S(2)}) %copy-start.3) | copy-done | bytes 524312
  4.2 0.0 copy-start.4
  4.2 0.0 copy-start.5
  4.2 52.6 %mixed_kernel.1 = bf16[12288,128]{1,0:T(8,128)(2,1)S(1)} custom-call(bf16[4096,128]{1,0:T(8,128)(2,1)S(1)} %copy-done.2, bf16[32,128,384]{2,1,0:T(8,128)(2,1)S(1)} %copy-done.1, bf16[512,512]{1,0:T(8,128)(2,1)S(1)} %copy-done.3), custom_call_target="tpu_custom_call" | custom-call | tf_op jit(solution)/shard_map/mixed_kernel/pallas_call | solution.py:199
  56.8 0.0 copy-done.4
  56.8 0.0 copy-done.5
  56.8 0.0 copy-start
  56.9 3.4 %copy-done = bf16[64,128,512]{2,1,0:T(8,128)(2,1)S(1)} copy-done((bf16[64,128,512]{2,1,0:T(8,128)(2,1)S(1)}, bf16[64,128,512]{2,1,0:T(8,128)(2,1)}, u32[]{:S(2)}) %copy-start) | copy-done | bytes 8388632
  60.2 5.6 %impute_kernel.1 = bf16[64,128,128]{2,1,0:T(8,128)(2,1)} custom-call(s32[64]{0:T(128)S(1)} %copy-done.4, s32[64]{0:T(128)S(1)} %copy-done.5, bf16[96,128,128]{2,1,0:T(8,128)(2,1)S(1)} %bitcast.2, bf16[64,128,512]{2,1,0:T(8,128)(2,1)S(1)} %copy-done), custom_call_target="tpu_custom_call" | custom-call | tf_op jit(solution)/shard_map/impute_kernel/pallas_call | solution.py:242
Async XLA Ops:
  0.0 1.9 %copy-start.1 = (bf16[32,128,384]{2,1,0:T(8,128)(2,1)S(1)}, bf16[32,128,384]{2,1,0:T(8,128)(2,1)}, u32[]{:S(2)}) copy-start(bf16[32,128,384]{2,1,0:T(8,128)(2,1)} %band_ref.1) | copy-start | bytes 9437188
  1.9 1.2 %copy-start.2 = (bf16[4096,128]{1,0:T(8,128)(2,1)S(1)}, bf16[4096,128]{1,0:T(8,128)(2,1)}, u32[]{:S(2)}) copy-start(bf16[4096,128]{1,0:T(8,128)(2,1)} %z_ref.1) | copy-start | bytes 3145732
  3.1 1.0 %copy-start.3 = (bf16[512,512]{1,0:T(8,128)(2,1)S(1)}, bf16[512,512]{1,0:T(8,128)(2,1)}, u32[]{:S(2)}) copy-start(bf16[512,512]{1,0:T(8,128)(2,1)} %mix_ref.1) | copy-start | bytes 1572868
  4.2 52.7 %copy-start.4 = (s32[64]{0:T(128)S(1)}, s32[64]{0:T(128)}, u32[]{:S(2)}) copy-start(s32[64]{0:T(128)} %start_ref.1) | copy-start | bytes 772
  4.2 52.7 %copy-start.5 = (s32[64]{0:T(128)S(1)}, s32[64]{0:T(128)}, u32[]{:S(2)}) copy-start(s32[64]{0:T(128)} %count_ref.1) | copy-start | bytes 772
  56.8 3.4 %copy-start = (bf16[64,128,512]{2,1,0:T(8,128)(2,1)S(1)}, bf16[64,128,512]{2,1,0:T(8,128)(2,1)}, u32[]{:S(2)}) copy-start(bf16[64,128,512]{2,1,0:T(8,128)(2,1)} %ld_ref.1) | copy-start | bytes 25165828

commit v2 on v1

--- a/solution.py
+++ b/solution.py
@@ -9,17 +9,31 @@
 
 BLK = 128
 WIN = 4
+HEAD_SIZES = (1, 1, 2, 2)
 CHUNK_BLOCKS = 4
-AHEAD = 2
+LAST_BLOCKS = 2
+AHEAD = 3
 UNTYPED_TILE = 8
 MESH = pl.DeviceIdType.MESH
 
 
+def chunk_plan(blocks):
+    plan = []
+    at = LAST_BLOCKS
+    sizes = list(HEAD_SIZES)
+    while at < blocks:
+        size = min(sizes.pop(0) if sizes else CHUNK_BLOCKS, blocks - at)
+        plan.append((at, size))
+        at += size
+    plan.append((0, LAST_BLOCKS))
+    return plan
+
+
 def mixed_kernel(
-    chunks, blocks, groups, var_size,
-    z_ref, band_ref, mix_ref, ext_ref,
+    plan, blocks, groups, var_size,
+    z_ref, band_ref, mix_ref, ld_ref, ext_ref, ldv_ref,
     zb, bandv, w, mv, mx,
-    z_sem, band_sem, mix_sem, own_sem, edge_send, edge_recv, xy_send, xy_recv, halo_send, halo_recv,
+    z_sem, ld_sem, band_sem, mix_sem, own_sem, edge_send, edge_recv, xy_send, xy_recv, halo_send, halo_recv,
 ):
     t = lax.axis_index("trait")
     g = lax.axis_index("sec") * var_size + lax.axis_index("var")
@@ -32,8 +46,10 @@
     left = {"sec": left_g // var_size, "var": lax.rem(left_g, var_size)}
     has_left, has_right = g > 0, g < groups - 1
     rows = blocks * BLK
-    chunk = CHUNK_BLOCKS * BLK
-    half = chunk // 2
+    order = range(len(plan))
+
+    def rows_of(c, offset=0):
+        return pl.ds(offset + plan[c][0] * BLK, plan[c][1] * BLK)
 
     barrier = pltpu.get_barrier_semaphore()
 
@@ -53,10 +69,8 @@
 
     load_z = pltpu.make_async_copy(z_ref, zb.at[pl.ds(BLK, rows)], z_sem)
     load_z.start()
-    order = [(i + 1) % chunks for i in range(chunks)]
-
     def load_band(c):
-        part = pl.ds(c * CHUNK_BLOCKS, CHUNK_BLOCKS)
+        part = pl.ds(*plan[c])
         return pltpu.make_async_copy(band_ref.at[part], bandv.at[part], band_sem.at[c])
 
     for c in order:
@@ -72,6 +86,7 @@
     ]
     for copy in load_mix:
         copy.start()
+    load_ld = pltpu.make_async_copy(ld_ref, ldv_ref, ld_sem)
 
     @pl.when(jnp.logical_not(has_left))
     def _():
@@ -90,51 +105,52 @@
 
     def whiten(c):
         load_band(c).wait()
-        if c == chunks - 1:
+        if sum(plan[c]) == blocks:
             pl.when(has_right)(edge_left.wait_recv)
-        if c == 0:
+        if plan[c][0] == 0:
             pl.when(has_left)(edge_right.wait_recv)
 
         def one(i, carry):
-            b = c * CHUNK_BLOCKS + i
+            b = plan[c][0] + i
             first = pl.multiple_of(b * BLK, BLK)
             sums = jnp.dot(bandv[b], zb[pl.ds(first, 3 * BLK), :], preferred_element_type=jnp.float32)
             w[0, pl.ds(first, BLK), :] = sums.astype(w.dtype)
             return carry
 
-        lax.fori_loop(0, CHUNK_BLOCKS, one, 0)
+        lax.fori_loop(0, plan[c][1], one, 0, unroll=True)
 
     def own_sends(c):
-        part = pl.ds(c * chunk, chunk)
+        part = rows_of(c)
         return (
             remote(w.at[0, part], w.at[1, part], xy_send.at[0, c], xy_recv.at[0, c], x_dev),
             remote(w.at[0, part], w.at[2, part], xy_send.at[1, c], xy_recv.at[1, c], y_dev),
         )
 
     def relays(c):
-        lower, upper = pl.ds(c * chunk, half), pl.ds(c * chunk + half, half)
+        first, half = plan[c][0] * BLK, plan[c][1] * BLK // 2
+        lower, upper = pl.ds(first, half), pl.ds(first + half, half)
         return (
             remote(w.at[1, lower], w.at[3, lower], xy_send.at[2, c], xy_recv.at[2, c], y_dev),
             remote(w.at[2, upper], w.at[3, upper], xy_send.at[3, c], xy_recv.at[3, c], x_dev),
         )
 
     def halos(c):
-        part = pl.ds(c * chunk, chunk)
+        part = rows_of(c)
         return (
             remote(mx.at[part], ext_ref.at[part], halo_send.at[0, c], halo_recv.at[0, c], right),
             remote(
-                mx.at[part], ext_ref.at[pl.ds(2 * rows + c * chunk, chunk)],
+                mx.at[part], ext_ref.at[rows_of(c, 2 * rows)],
                 halo_send.at[1, c], halo_recv.at[1, c], left,
             ),
         )
 
     def keep(c):
         return pltpu.make_async_copy(
-            mx.at[pl.ds(c * chunk, chunk)], ext_ref.at[pl.ds(rows + c * chunk, chunk)], own_sem.at[c]
+            mx.at[rows_of(c)], ext_ref.at[rows_of(c, rows)], own_sem.at[c]
         )
 
     def mix(c):
-        part = pl.ds(c * chunk, chunk)
+        part = rows_of(c)
         all_traits = jnp.concatenate([w[j, part, :] for j in range(4)], axis=1)
         sums = jnp.dot(all_traits, mv[...], preferred_element_type=jnp.float32)
         mx[part, :] = sums.astype(mx.dtype)
@@ -148,8 +164,10 @@
     for c in order[:AHEAD]:
         for copy in own_sends(c):
             copy.start()
+    load_ld.start()
     for copy in load_mix:
         copy.wait()
+    chunks = len(plan)
     for i in range(chunks + 1):
         if i < chunks:
             for copy in own_sends(order[i]):
@@ -186,28 +204,30 @@
             to_left.wait_send()
             to_right.wait_recv()
 
+    load_ld.wait()
     pl.when(has_right)(edge_right.wait_send)
     pl.when(has_left)(edge_left.wait_send)
 
 
-def mixed_with_neighbours(z_typed, band_inverse, trait_mix, groups, var_size):
+def mixed_with_neighbours(z_typed, band_inverse, trait_mix, ld_untyped, groups, var_size):
     rows = z_typed.shape[0]
     blocks = rows // BLK
-    chunks = blocks // CHUNK_BLOCKS
+    plan = chunk_plan(blocks)
+    chunks = len(plan)
     dma = pltpu.SemaphoreType.DMA
     kind = z_typed.dtype
     return pl.pallas_call(
-        functools.partial(mixed_kernel, chunks, blocks, groups, var_size),
-        out_shape=jax.ShapeDtypeStruct((3 * rows, BLK), kind),
-        in_specs=[pl.BlockSpec(memory_space=pl.ANY)] * 3,
-        out_specs=pl.BlockSpec(memory_space=pl.ANY),
+        functools.partial(mixed_kernel, plan, blocks, groups, var_size),
+        out_shape=(pltpu.VMEM((3 * rows, BLK), kind), pltpu.VMEM(ld_untyped.shape, kind)),
+        in_specs=[pl.BlockSpec(memory_space=pl.ANY)] * 4,
+        out_specs=(pl.BlockSpec(memory_space=pl.ANY),) * 2,
         scratch_shapes=[
             pltpu.VMEM((rows + 2 * BLK, BLK), kind),
             pltpu.VMEM(band_inverse.shape, kind),
             pltpu.VMEM((4, rows, BLK), kind),
             pltpu.VMEM((4 * BLK, BLK), kind),
             pltpu.VMEM((rows, BLK), kind),
-            dma, dma((chunks,)), dma((4,)), dma((chunks,)),
+            dma, dma, dma((chunks,)), dma((4,)), dma((chunks,)),
             dma((2,)), dma((2,)),
             dma((4, chunks)), dma((4, chunks)),
             dma((2, chunks)), dma((2, chunks)),
@@ -216,12 +236,12 @@
             collective_id=0, has_side_effects=True, vmem_limit_bytes=16 * 1024 * 1024
         ),
         name="mixed_kernel",
-    )(z_typed, band_inverse, trait_mix)
+    )(*(pltpu.with_memory_space_constraint(v, pltpu.HBM) for v in (z_typed, band_inverse, trait_mix, ld_untyped)))
 
 
 def impute_kernel(blocks, var_size, start_ref, count_ref, ext_ref, ld_ref, out_ref):
     g = lax.axis_index("sec") * var_size + lax.axis_index("var")
-    tile = ld_ref.shape[0]
+    tile = out_ref.shape[0]
     first = pl.program_id(0) * tile
     for i in range(tile):
         start = start_ref[first + i] - (g - 1) * blocks
@@ -231,7 +251,7 @@
             block = ext_ref[jnp.clip(start + s, 0, 3 * blocks - 1)]
             parts.append(jnp.where(s < count, block, jnp.zeros_like(block)))
         window = jnp.concatenate(parts, axis=0)
-        sums = jnp.dot(ld_ref[i], window, preferred_element_type=jnp.float32)
+        sums = jnp.dot(ld_ref[first + i], window, preferred_element_type=jnp.float32)
         out_ref[i] = sums.astype(out_ref.dtype)
 
 
@@ -245,8 +265,8 @@
             num_scalar_prefetch=2,
             grid=(untyped // UNTYPED_TILE,),
             in_specs=[
-                pl.BlockSpec((total, BLK, cols), lambda i, *_: (0, 0, 0)),
-                pl.BlockSpec((UNTYPED_TILE,) + ld_untyped.shape[1:], lambda i, *_: (i, 0, 0)),
+                pl.BlockSpec(memory_space=pltpu.VMEM),
+                pl.BlockSpec(memory_space=pltpu.VMEM),
             ],
             out_specs=pl.BlockSpec((UNTYPED_TILE, BLK, cols), lambda i, *_: (i, 0, 0)),
         ),
@@ -257,8 +277,8 @@
 
 
 def on_device(groups, var_size, z_typed, band_inverse, ld_untyped, trait_mix, win_start, win_count):
-    ext = mixed_with_neighbours(z_typed, band_inverse, trait_mix, groups, var_size)
-    imputed = impute(ext, ld_untyped, win_start, win_count, var_size)
+    ext, ld_near = mixed_with_neighbours(z_typed, band_inverse, trait_mix, ld_untyped, groups, var_size)
+    imputed = impute(ext, ld_near, win_start, win_count, var_size)
     return imputed.reshape(ld_untyped.shape[0] * BLK, z_typed.shape[1])
 
 

time: 66.1 us -> 62.2 us (0.941)
  local copies, waits for them, and re-layouts: 7.54 us -> 0.01 us
  Pallas kernels: 58.3 us -> 62 us
    unnamed x12 -> x4, local copies, waits for them, and re-layouts: 7.54 us -> 0.01 us
    pallas_call x1, Pallas kernels: 52.6 us -> 56.4 us  [mixed_with_neighbours(): pl.pallas_call(functools.partial(mixed_kernel, plan, blocks, groups, var_...]
where the time goes in v2:
time: 62.2 us; the launch traced here: 62.1 us
  Pallas kernels  62 us (100%)
    pallas_call x1, Pallas kernels, mixed_with_neighbours(): pl.pallas_call(functools.partial(mixed_kernel, plan, blocks, groups, var_...  56.4 us
    pallas_call x1, Pallas kernels, impute(): pl.pallas_call(functools.partial(impute_kernel, total // 3, var_size), gr...  5.64 us

profile of v2, /device:TPU:1, one launch (start us, length us, event | category | flops | bytes accessed | tf_op | source)
XLA Modules:
  0.0 62.1 jit_solution(4907075632766010026)
XLA Ops:
  0.0 0.0 copy-start.1
  0.0 0.0 copy-start
  0.0 56.4 %mixed_kernel.1 = (bf16[12288,128]{1,0:T(8,128)(2,1)S(1)}, bf16[64,128,512]{2,1,0:T(8,128)(2,1)S(1)}) custom-call(bf16[4096,128]{1,0:T(8,128)(2,1)} %z_ref.1, bf16[32,128,384]{2,1,0:T(8,128)(2,1)} %band_ref.1, bf16[512,512]{1,0:T(8,128)(2,1)} %mix_ref.1, bf16[64,128,512]{2,1,0:T(8,128)(2,1)} %ld_ref.1), custom_call_target="tpu_custom_call" | custom-call | tf_op jit(solution)/shard_map/mixed_kernel/pallas_call | solution.py:219
  56.4 0.0 copy-done.1
  56.4 0.0 copy-done
  56.4 5.6 %impute_kernel.1 = bf16[64,128,128]{2,1,0:T(8,128)(2,1)} custom-call(s32[64]{0:T(128)S(1)} %copy-done, s32[64]{0:T(128)S(1)} %copy-done.1, bf16[96,128,128]{2,1,0:T(8,128)(2,1)S(1)} %bitcast.2, bf16[64,128,512]{2,1,0:T(8,128)(2,1)S(1)} %get-tuple-element.8.ld_ref), custom_call_target="tpu_custom_call" | custom-call | tf_op jit(solution)/shard_map/impute_kernel/pallas_call | solution.py:262
Async XLA Ops:
  0.0 56.4 %copy-start.1 = (s32[64]{0:T(128)S(1)}, s32[64]{0:T(128)}, u32[]{:S(2)}) copy-start(s32[64]{0:T(128)} %count_ref.1) | copy-start | bytes 772
  0.0 56.4 %copy-start = (s32[64]{0:T(128)S(1)}, s32[64]{0:T(128)}, u32[]{:S(2)}) copy-start(s32[64]{0:T(128)} %start_ref.1) | copy-start | bytes 772

commit v3 on v2

--- a/solution.py
+++ b/solution.py
@@ -9,10 +9,11 @@
 
 BLK = 128
 WIN = 4
-HEAD_SIZES = (1, 1, 2, 2)
-CHUNK_BLOCKS = 4
+HEAD_SIZES = ()
+CHUNK_BLOCKS = 2
 LAST_BLOCKS = 2
 AHEAD = 3
+LAG = 2
 UNTYPED_TILE = 8
 MESH = pl.DeviceIdType.MESH
 
@@ -32,15 +33,16 @@
 def mixed_kernel(
     plan, blocks, groups, var_size,
     z_ref, band_ref, mix_ref, ld_ref, ext_ref, ldv_ref,
-    zb, bandv, w, mv, mx,
-    z_sem, ld_sem, band_sem, mix_sem, own_sem, edge_send, edge_recv, xy_send, xy_recv, halo_send, halo_recv,
+    zb, bandv, w, gathered, mv, results, mx,
+    z_sem, ld_sem, band_sem, mix_sem, own_sem, edge_send, edge_recv, in_send, in_recv, out_send, out_recv, halo_send, halo_recv,
 ):
     t = lax.axis_index("trait")
     g = lax.axis_index("sec") * var_size + lax.axis_index("var")
     x_peer = t + 1 - 2 * lax.rem(t, 2)
     y_peer = t + 2 - 4 * (t // 2)
     far_peer = x_peer + y_peer - t
-    x_dev, y_dev = {"trait": x_peer}, {"trait": y_peer}
+    peers = (t, x_peer, y_peer, far_peer)
+    others = range(1, len(peers))
     right = {"sec": (g + 1) // var_size, "var": lax.rem(g + 1, var_size)}
     left_g = lax.rem(g + groups - 1, groups)
     left = {"sec": left_g // var_size, "var": lax.rem(left_g, var_size)}
@@ -56,8 +58,8 @@
     def greet(device):
         pl.semaphore_signal(barrier, inc=1, device_id=device, device_id_type=MESH)
 
-    greet(x_dev)
-    greet(y_dev)
+    for j in others:
+        greet({"trait": peers[j]})
     pl.when(has_left)(lambda: greet(left))
     pl.when(has_right)(lambda: greet(right))
 
@@ -75,14 +77,16 @@
 
     for c in order:
         load_band(c).start()
-    columns = pl.ds(pl.multiple_of(t * BLK, BLK), BLK)
     load_mix = [
         pltpu.make_async_copy(
-            mix_ref.at[pl.ds(pl.multiple_of(peer * BLK, BLK), BLK), columns],
-            mv.at[pl.ds(j * BLK, BLK)],
-            mix_sem.at[j],
-        )
-        for j, peer in enumerate((t, x_peer, y_peer, far_peer))
+            mix_ref.at[
+                pl.ds(pl.multiple_of(taken * BLK, BLK), BLK), pl.ds(pl.multiple_of(given * BLK, BLK), BLK)
+            ],
+            mv.at[pl.ds(i * BLK, BLK), pl.ds(j * BLK, BLK)],
+            mix_sem.at[i, j],
+        )
+        for i, taken in enumerate(peers)
+        for j, given in enumerate(peers)
     ]
     for copy in load_mix:
         copy.start()
@@ -114,25 +118,44 @@
             b = plan[c][0] + i
             first = pl.multiple_of(b * BLK, BLK)
             sums = jnp.dot(bandv[b], zb[pl.ds(first, 3 * BLK), :], preferred_element_type=jnp.float32)
-            w[0, pl.ds(first, BLK), :] = sums.astype(w.dtype)
+            w[pl.ds(first, BLK), :] = sums.astype(w.dtype)
             return carry
 
         lax.fori_loop(0, plan[c][1], one, 0, unroll=True)
 
-    def own_sends(c):
-        part = rows_of(c)
-        return (
-            remote(w.at[0, part], w.at[1, part], xy_send.at[0, c], xy_recv.at[0, c], x_dev),
-            remote(w.at[0, part], w.at[2, part], xy_send.at[1, c], xy_recv.at[1, c], y_dev),
-        )
-
-    def relays(c):
-        first, half = plan[c][0] * BLK, plan[c][1] * BLK // 2
-        lower, upper = pl.ds(first, half), pl.ds(first + half, half)
-        return (
-            remote(w.at[1, lower], w.at[3, lower], xy_send.at[2, c], xy_recv.at[2, c], y_dev),
-            remote(w.at[2, upper], w.at[3, upper], xy_send.at[3, c], xy_recv.at[3, c], x_dev),
-        )
+    def part_of(c, peer):
+        part = plan[c][1] * BLK // len(peers)
+        return pl.ds(pl.multiple_of(plan[c][0] * BLK + peer * part, part), part)
+
+    def share_of(c):
+        return pl.ds(plan[c][0] * BLK // len(peers), plan[c][1] * BLK // len(peers))
+
+    def sends_in(c):
+        return [
+            remote(
+                w.at[part_of(c, peers[j])], gathered.at[j - 1, share_of(c)],
+                in_send.at[j - 1, c], in_recv.at[j - 1, c], {"trait": peers[j]},
+            )
+            for j in others
+        ]
+
+    def sends_out(c):
+        return [
+            remote(
+                results.at[j - 1, share_of(c)], mx.at[part_of(c, t)],
+                out_send.at[j - 1, c], out_recv.at[j - 1, c], {"trait": peers[j]},
+            )
+            for j in others
+        ]
+
+    def arrivals(c):
+        return [
+            remote(
+                results.at[j - 1, share_of(c)], mx.at[part_of(c, peers[j])],
+                out_send.at[j - 1, c], out_recv.at[j - 1, c], {"trait": peers[j]},
+            )
+            for j in others
+        ]
 
     def halos(c):
         part = rows_of(c)
@@ -150,46 +173,49 @@
         )
 
     def mix(c):
-        part = rows_of(c)
-        all_traits = jnp.concatenate([w[j, part, :] for j in range(4)], axis=1)
-        sums = jnp.dot(all_traits, mv[...], preferred_element_type=jnp.float32)
-        mx[part, :] = sums.astype(mx.dtype)
+        all_traits = jnp.concatenate(
+            [w[part_of(c, t), :]] + [gathered[j - 1, share_of(c), :] for j in others], axis=1
+        )
+        sums = jnp.dot(all_traits, mv[...], preferred_element_type=jnp.float32).astype(mx.dtype)
+        mx[part_of(c, t), :] = sums[:, :BLK]
+        for j in others:
+            results[j - 1, share_of(c), :] = sums[:, j * BLK : (j + 1) * BLK]
 
     load_z.wait()
     for c in order[: AHEAD + 1]:
         whiten(c)
-    pl.semaphore_wait(barrier, 2 + has_left.astype(jnp.int32) + has_right.astype(jnp.int32))
+    pl.semaphore_wait(barrier, len(others) + has_left.astype(jnp.int32) + has_right.astype(jnp.int32))
     pl.when(has_right)(edge_right.start)
     pl.when(has_left)(edge_left.start)
     for c in order[:AHEAD]:
-        for copy in own_sends(c):
+        for copy in sends_in(c):
             copy.start()
     load_ld.start()
     for copy in load_mix:
         copy.wait()
     chunks = len(plan)
-    for i in range(chunks + 1):
+    for i in range(chunks + LAG):
         if i < chunks:
-            for copy in own_sends(order[i]):
+            for copy in sends_in(i):
                 copy.wait_recv()
-            for copy in relays(order[i]):
+            mix(i)
+            for copy in sends_out(i):
                 copy.start()
-            if i + AHEAD < chunks:
-                for copy in own_sends(order[i + AHEAD]):
-                    copy.start()
-        if i >= 1:
-            c = order[i - 1]
-            for copy in relays(c):
+        if i + AHEAD < chunks:
+            for copy in sends_in(i + AHEAD):
+                copy.start()
+        if i >= LAG:
+            c = i - LAG
+            for copy in arrivals(c):
                 copy.wait_recv()
-            mix(c)
             to_right, to_left = halos(c)
             pl.when(has_right)(to_right.start)
             pl.when(has_left)(to_left.start)
             keep(c).start()
         if i + AHEAD + 1 < chunks:
-            whiten(order[i + AHEAD + 1])
+            whiten(i + AHEAD + 1)
     for c in order:
-        for copy in own_sends(c) + relays(c):
+        for copy in sends_in(c) + sends_out(c):
             copy.wait_send()
         keep(c).wait()
         to_right, to_left = halos(c)
@@ -213,6 +239,7 @@
     rows = z_typed.shape[0]
     blocks = rows // BLK
     plan = chunk_plan(blocks)
+    peers = trait_mix.shape[0] // BLK
     chunks = len(plan)
     dma = pltpu.SemaphoreType.DMA
     kind = z_typed.dtype
@@ -224,12 +251,15 @@
         scratch_shapes=[
             pltpu.VMEM((rows + 2 * BLK, BLK), kind),
             pltpu.VMEM(band_inverse.shape, kind),
-            pltpu.VMEM((4, rows, BLK), kind),
-            pltpu.VMEM((4 * BLK, BLK), kind),
             pltpu.VMEM((rows, BLK), kind),
-            dma, dma, dma((chunks,)), dma((4,)), dma((chunks,)),
+            pltpu.VMEM((peers - 1, rows // peers, BLK), kind),
+            pltpu.VMEM(trait_mix.shape, kind),
+            pltpu.VMEM((peers - 1, rows // peers, BLK), kind),
+            pltpu.VMEM((rows, BLK), kind),
+            dma, dma, dma((chunks,)), dma((peers, peers)), dma((chunks,)),
             dma((2,)), dma((2,)),
-            dma((4, chunks)), dma((4, chunks)),
+            dma((peers - 1, chunks)), dma((peers - 1, chunks)),
+            dma((peers - 1, chunks)), dma((peers - 1, chunks)),
             dma((2, chunks)), dma((2, chunks)),
         ],
         compiler_params=pltpu.CompilerParams(

time: 62.2 us -> 56.2 us (0.904)
  Pallas kernels: 62 us -> 56 us
    pallas_call x1, Pallas kernels: 56.4 us -> 50.4 us  [mixed_with_neighbours(): pl.pallas_call(functools.partial(mixed_kernel, plan, blocks, groups, var_...]
where the time goes in v3:
time: 56.2 us; the launch traced here: 56.1 us
  Pallas kernels  56 us (100%)
    pallas_call x1, Pallas kernels, mixed_with_neighbours(): pl.pallas_call(functools.partial(mixed_kernel, plan, blocks, groups, var_...  50.4 us
    pallas_call x1, Pallas kernels, impute(): pl.pallas_call(functools.partial(impute_kernel, total // 3, var_size), gr...  5.63 us

profile of v3, /device:TPU:1, one launch (start us, length us, event | category | flops | bytes accessed | tf_op | source)
XLA Modules:
  0.0 56.1 jit_solution(7714954174016109283)
XLA Ops:
  0.0 0.0 copy-start.1
  0.0 0.0 copy-start
  0.0 50.4 %mixed_kernel.1 = (bf16[12288,128]{1,0:T(8,128)(2,1)S(1)}, bf16[64,128,512]{2,1,0:T(8,128)(2,1)S(1)}) custom-call(bf16[4096,128]{1,0:T(8,128)(2,1)} %z_ref.1, bf16[32,128,384]{2,1,0:T(8,128)(2,1)} %band_ref.1, bf16[512,512]{1,0:T(8,128)(2,1)} %mix_ref.1, bf16[64,128,512]{2,1,0:T(8,128)(2,1)} %ld_ref.1), custom_call_target="tpu_custom_call" | custom-call | tf_op jit(solution)/shard_map/mixed_kernel/pallas_call | solution.py:246
  50.4 0.0 copy-done.1
  50.4 0.0 copy-done
  50.4 5.6 %impute_kernel.1 = bf16[64,128,128]{2,1,0:T(8,128)(2,1)} custom-call(s32[64]{0:T(128)S(1)} %copy-done, s32[64]{0:T(128)S(1)} %copy-done.1, bf16[96,128,128]{2,1,0:T(8,128)(2,1)S(1)} %bitcast.2, bf16[64,128,512]{2,1,0:T(8,128)(2,1)S(1)} %get-tuple-element.8.ld_ref), custom_call_target="tpu_custom_call" | custom-call | tf_op jit(solution)/shard_map/impute_kernel/pallas_call | solution.py:292
Async XLA Ops:
  0.0 50.4 %copy-start.1 = (s32[64]{0:T(128)S(1)}, s32[64]{0:T(128)}, u32[]{:S(2)}) copy-start(s32[64]{0:T(128)} %count_ref.1) | copy-start | bytes 772
  0.0 50.4 %copy-start = (s32[64]{0:T(128)S(1)}, s32[64]{0:T(128)}, u32[]{:S(2)}) copy-start(s32[64]{0:T(128)} %start_ref.1) | copy-start | bytes 772

commit v4 on v3

--- a/solution.py
+++ b/solution.py
@@ -14,7 +14,7 @@
 LAST_BLOCKS = 2
 AHEAD = 3
 LAG = 2
-UNTYPED_TILE = 8
+UNTYPED_TILE = 32
 MESH = pl.DeviceIdType.MESH
 
 

time: 56.2 us -> 54.7 us (0.973)
  Pallas kernels: 56 us -> 54.5 us
    pallas_call x1, Pallas kernels: 5.63 us -> 4.1 us  [impute(): pl.pallas_call(functools.partial(impute_kernel, total // 3, var_size), gr...]
where the time goes in v4:
time: 54.7 us; the launch traced here: 54.5 us
  Pallas kernels  54.5 us (100%)
    pallas_call x1, Pallas kernels, mixed_with_neighbours(): pl.pallas_call(functools.partial(mixed_kernel, plan, blocks, groups, var_...  50.4 us
    pallas_call x1, Pallas kernels, impute(): pl.pallas_call(functools.partial(impute_kernel, total // 3, var_size), gr...  4.1 us

profile of v4, /device:TPU:1, one launch (start us, length us, event | category | flops | bytes accessed | tf_op | source)
XLA Modules:
  0.0 54.5 jit_solution(17870695698632635933)
XLA Ops:
  0.0 0.0 copy-start.1
  0.0 0.0 copy-start
  0.0 50.4 %mixed_kernel.1 = (bf16[12288,128]{1,0:T(8,128)(2,1)S(1)}, bf16[64,128,512]{2,1,0:T(8,128)(2,1)S(1)}) custom-call(bf16[4096,128]{1,0:T(8,128)(2,1)} %z_ref.1, bf16[32,128,384]{2,1,0:T(8,128)(2,1)} %band_ref.1, bf16[512,512]{1,0:T(8,128)(2,1)} %mix_ref.1, bf16[64,128,512]{2,1,0:T(8,128)(2,1)} %ld_ref.1), custom_call_target="tpu_custom_call" | custom-call | tf_op jit(solution)/shard_map/mixed_kernel/pallas_call | solution.py:246
  50.4 0.0 copy-done.1
  50.4 0.0 copy-done
  50.4 4.1 %impute_kernel.1 = bf16[64,128,128]{2,1,0:T(8,128)(2,1)} custom-call(s32[64]{0:T(128)S(1)} %copy-done, s32[64]{0:T(128)S(1)} %copy-done.1, bf16[96,128,128]{2,1,0:T(8,128)(2,1)S(1)} %bitcast.2, bf16[64,128,512]{2,1,0:T(8,128)(2,1)S(1)} %get-tuple-element.8.ld_ref), custom_call_target="tpu_custom_call" | custom-call | tf_op jit(solution)/shard_map/impute_kernel/pallas_call | solution.py:292
Async XLA Ops:
  0.0 50.4 %copy-start.1 = (s32[64]{0:T(128)S(1)}, s32[64]{0:T(128)}, u32[]{:S(2)}) copy-start(s32[64]{0:T(128)} %count_ref.1) | copy-start | bytes 772
  0.0 50.4 %copy-start = (s32[64]{0:T(128)S(1)}, s32[64]{0:T(128)}, u32[]{:S(2)}) copy-start(s32[64]{0:T(128)} %start_ref.1) | copy-start | bytes 772

commit v5 on v4

--- a/solution.py
+++ b/solution.py
@@ -10,10 +10,10 @@
 BLK = 128
 WIN = 4
 HEAD_SIZES = ()
-CHUNK_BLOCKS = 2
+CHUNK_BLOCKS = 4
 LAST_BLOCKS = 2
-AHEAD = 3
-LAG = 2
+AHEAD = 2
+LAG = 1
 UNTYPED_TILE = 32
 MESH = pl.DeviceIdType.MESH
 
@@ -157,15 +157,19 @@
             for j in others
         ]
 
-    def halos(c):
-        part = rows_of(c)
+    def halos(c, j):
+        part = plan[c][1] * BLK // len(peers)
+        above = pl.ds(pl.multiple_of(2 * rows + plan[c][0] * BLK + peers[j] * part, part), part)
+        mine = part_of(c, peers[j])
         return (
-            remote(mx.at[part], ext_ref.at[part], halo_send.at[0, c], halo_recv.at[0, c], right),
-            remote(
-                mx.at[part], ext_ref.at[rows_of(c, 2 * rows)],
-                halo_send.at[1, c], halo_recv.at[1, c], left,
-            ),
-        )
+            remote(mx.at[mine], ext_ref.at[mine], halo_send.at[0, j, c], halo_recv.at[0, j, c], right),
+            remote(mx.at[mine], ext_ref.at[above], halo_send.at[1, j, c], halo_recv.at[1, j, c], left),
+        )
+
+    def send_halos(c, j):
+        to_right, to_left = halos(c, j)
+        pl.when(has_right)(to_right.start)
+        pl.when(has_left)(to_left.start)
 
     def keep(c):
         return pltpu.make_async_copy(
@@ -201,16 +205,15 @@
             mix(i)
             for copy in sends_out(i):
                 copy.start()
+            send_halos(i, 0)
         if i + AHEAD < chunks:
             for copy in sends_in(i + AHEAD):
                 copy.start()
         if i >= LAG:
             c = i - LAG
-            for copy in arrivals(c):
+            for j, copy in zip(others, arrivals(c)):
                 copy.wait_recv()
-            to_right, to_left = halos(c)
-            pl.when(has_right)(to_right.start)
-            pl.when(has_left)(to_left.start)
+                send_halos(c, j)
             keep(c).start()
         if i + AHEAD + 1 < chunks:
             whiten(i + AHEAD + 1)
@@ -218,17 +221,19 @@
         for copy in sends_in(c) + sends_out(c):
             copy.wait_send()
         keep(c).wait()
-        to_right, to_left = halos(c)
+        every = [halos(c, j) for j in range(len(peers))]
 
         @pl.when(has_right)
         def _():
-            to_right.wait_send()
-            to_left.wait_recv()
+            for to_right, to_left in every:
+                to_right.wait_send()
+                to_left.wait_recv()
 
         @pl.when(has_left)
         def _():
-            to_left.wait_send()
-            to_right.wait_recv()
+            for to_right, to_left in every:
+                to_left.wait_send()
+                to_right.wait_recv()
 
     load_ld.wait()
     pl.when(has_right)(edge_right.wait_send)
@@ -260,7 +265,7 @@
             dma((2,)), dma((2,)),
             dma((peers - 1, chunks)), dma((peers - 1, chunks)),
             dma((peers - 1, chunks)), dma((peers - 1, chunks)),
-            dma((2, chunks)), dma((2, chunks)),
+            dma((2, peers, chunks)), dma((2, peers, chunks)),
         ],
         compiler_params=pltpu.CompilerParams(
             collective_id=0, has_side_effects=True, vmem_limit_bytes=16 * 1024 * 1024

time: 54.7 us -> 54.2 us (level)
  no operation moved by 1% of the time
where the time goes in v5:
time: 54.2 us; the launch traced here: 54 us
  Pallas kernels  54 us (100%)
    pallas_call x1, Pallas kernels, mixed_with_neighbours(): pl.pallas_call(functools.partial(mixed_kernel, plan, blocks, groups, var_...  49.9 us
    pallas_call x1, Pallas kernels, impute(): pl.pallas_call(functools.partial(impute_kernel, total // 3, var_size), gr...  4.09 us

profile of v5, /device:TPU:1, one launch (start us, length us, event | category | flops | bytes accessed | tf_op | source)
XLA Modules:
  0.0 54.0 jit_solution(11449306717417890636)
XLA Ops:
  0.0 0.0 copy-start.1
  0.0 0.0 copy-start
  0.0 49.9 %mixed_kernel.1 = (bf16[12288,128]{1,0:T(8,128)(2,1)S(1)}, bf16[64,128,512]{2,1,0:T(8,128)(2,1)S(1)}) custom-call(bf16[4096,128]{1,0:T(8,128)(2,1)} %z_ref.1, bf16[32,128,384]{2,1,0:T(8,128)(2,1)} %band_ref.1, bf16[512,512]{1,0:T(8,128)(2,1)} %mix_ref.1, bf16[64,128,512]{2,1,0:T(8,128)(2,1)} %ld_ref.1), custom_call_target="tpu_custom_call" | custom-call | tf_op jit(solution)/shard_map/mixed_kernel/pallas_call | solution.py:251
  49.9 0.0 copy-done.1
  49.9 0.0 copy-done
  49.9 4.1 %impute_kernel.1 = bf16[64,128,128]{2,1,0:T(8,128)(2,1)} custom-call(s32[64]{0:T(128)S(1)} %copy-done, s32[64]{0:T(128)S(1)} %copy-done.1, bf16[96,128,128]{2,1,0:T(8,128)(2,1)S(1)} %bitcast.2, bf16[64,128,512]{2,1,0:T(8,128)(2,1)S(1)} %get-tuple-element.8.ld_ref), custom_call_target="tpu_custom_call" | custom-call | tf_op jit(solution)/shard_map/impute_kernel/pallas_call | solution.py:297
Async XLA Ops:
  0.0 49.9 %copy-start.1 = (s32[64]{0:T(128)S(1)}, s32[64]{0:T(128)}, u32[]{:S(2)}) copy-start(s32[64]{0:T(128)} %count_ref.1) | copy-start | bytes 772
  0.0 49.9 %copy-start = (s32[64]{0:T(128)S(1)}, s32[64]{0:T(128)}, u32[]{:S(2)}) copy-start(s32[64]{0:T(128)} %start_ref.1) | copy-start | bytes 772
